TPU v7x, 256 devices: a whole 4x4x8 slice. The times are simulated.
256 devices in a mesh: sec: 2 (over core), row: 4 (over x), col: 32 (over z, y).
Axes of the slice: x: 4, y: 4, z: 8, core: 2. Of those that a mesh axis runs over, the one named last changes fastest.
Arguments:
- leaf_rhs: bfloat16 [2, 4, 1, 32, 128, 256], P('sec', 'row', None, 'col'), may hold values from -6 to 6
- sep_rhs: bfloat16 [2, 4, 32, 128, 256], P('sec', 'row', 'col'), may hold values from -6 to 6
- top_rhs: bfloat16 [4, 32, 128, 256], P('row', 'col'), may hold values from -6 to 6
- leaf_inv: float32 [2, 4, 1, 32, 128, 128], P('sec', 'row', None, 'col'), may hold values from -1 to 3, as said below
- sep_inv: float32 [2, 4, 32, 128, 128], P('sec', 'row', 'col'), may hold values from -1 to 3, as said below
- top_inv: float32 [4, 32, 128, 128], P('row', 'col'), may hold values from -1 to 3, as said below
- sep_leaf: bfloat16 [2, 4, 32, 128, 4, 1, 32, 128], P('sec', 'row', None, None, None, None, 'col'), may hold values from -0.0625 to 0.0625
- top_leaf: bfloat16 [2, 4, 32, 128, 4, 1, 32, 128], P('sec', 'row', None, None, None, None, 'col'), may hold values from -0.046875 to 0.046875
- top_sep: bfloat16 [2, 4, 32, 128, 4, 32, 128], P('sec', 'row', None, None, None, 'col'), may hold values from -0.046875 to 0.046875
- sep_leaf_mask: int32 [2, 4, 32, 4, 1, 32], P('sec', 'row', None, None, None, 'col'), may hold values 0 or 1
- top_leaf_mask: int32 [2, 4, 32, 4, 1, 32], P('sec', 'row', None, None, None, 'col'), may hold values 0 or 1
- top_sep_mask: int32 [2, 4, 32, 4, 32], P('sec', 'row', None, None, 'col'), may hold values 0 or 1
Outputs:
- leaf_x: float32 [2, 4, 1, 32, 128, 256], P('sec', 'row', None, 'col')
- sep_x: float32 [2, 4, 32, 128, 256], P('sec', 'row', 'col')
- top_x: float32 [4, 32, 128, 256], P('row', 'col')
Inputs may be any that keep to these rules, and one draw needn't show every extreme that they name: `leaf_inv`: every 128 x 128 block is lower triangular with positive diagonal. `sep_inv`: every 128 x 128 block is lower triangular with positive diagonal. `top_inv`: every 128 x 128 block is lower triangular with positive diagonal.
All inputs are finite; a program needn't handle non-finite values. No bound on the sum of `sep_leaf_mask` or of `top_leaf_mask` or of `top_sep_mask` on one device may be relied on, other than what follows from the above.
Results may differ from a plain program's by a relative error of at most 0.0036.
Values may be sent and summed in bfloat16 or wider, within the bound.
A program may use at most 128 MiB of HBM per device.

v0:
```python
import jax
import jax.numpy as jnp
from jax import lax
from jax.sharding import PartitionSpec as P


def lower_apply(inverse, right_side):
    return jnp.einsum("...ab,...bn->...an", inverse, right_side, precision=lax.Precision.HIGHEST)


def upper_apply(inverse, right_side):
    return jnp.einsum("...ba,...bn->...an", inverse, right_side, precision=lax.Precision.HIGHEST)


def mask_tiles(tile_set, pattern):
    return tile_set * pattern.astype(jnp.bfloat16)[:, None, :, :, None]


def spread_down(values, update, totals):
    return update(totals, lax.all_gather(values, "row", axis=0, tiled=True), jnp.int32(0))


def reduce_row(partial_value, rhs_cols):
    col_count = lax.axis_size("col")
    summed = lax.psum_scatter(
        partial_value.reshape(col_count, partial_value.shape[0] // col_count, rhs_cols),
        "col",
        scatter_dimension=0,
        tiled=True,
    )
    return summed.reshape(summed.shape[1], rhs_cols)


def add_sections(partial_value):
    return lax.psum(partial_value, "sec")


def spread_across(values):
    return lax.all_gather(values[None], "col", axis=0, tiled=True)


def collect_up(term_fn, row_span):
    return lax.psum_scatter(
        term_fn(jnp.int32(0), row_span * lax.axis_size("row")),
        "row",
        scatter_dimension=0,
        tiled=True,
    )


def body(
    leaf_rhs,
    sep_rhs,
    top_rhs,
    leaf_inv,
    sep_inv,
    top_inv,
    sep_leaf,
    top_leaf,
    top_sep,
    sep_leaf_mask,
    top_leaf_mask,
    top_sep_mask,
):
    leaf_count = leaf_rhs.shape[2]
    tile_width = leaf_rhs.shape[4]
    rhs_cols = leaf_rhs.shape[5]
    col_count = sep_leaf.shape[2]
    row_count = sep_leaf.shape[4]
    rows_out = col_count * tile_width
    leaf_span = leaf_count * tile_width
    contract = (((0,), (0,)), ((), ()))
    sep_tiles = mask_tiles(sep_leaf[0, 0, :, :, :, :, 0], sep_leaf_mask[0, 0, :, :, :, 0])
    top_tiles = mask_tiles(top_leaf[0, 0, :, :, :, :, 0], top_leaf_mask[0, 0, :, :, :, 0])
    cross_tiles = (
        top_sep[0, 0, :, :, :, 0]
        * top_sep_mask[0, 0, :, :, 0].astype(jnp.bfloat16)[:, None, :, None]
    )
    leaf_y = lower_apply(leaf_inv[0, 0, :, 0], leaf_rhs[0, 0, :, 0].astype(jnp.float32))
    leaf_send = leaf_y.astype(jnp.bfloat16)

    def leaf_update(totals, pieces, offset):
        how_many = pieces.shape[0]
        flat_values = pieces.reshape(how_many * leaf_span, rhs_cols)
        sep_block = sep_tiles.reshape(rows_out, how_many * leaf_span)
        top_block = top_tiles.reshape(rows_out, how_many * leaf_span)
        return (
            jnp.dot(sep_block, flat_values, preferred_element_type=jnp.float32),
            jnp.dot(top_block, flat_values, preferred_element_type=jnp.float32),
        )

    empty_sum = jnp.zeros((rows_out, rhs_cols), jnp.float32)
    sep_part, top_part = spread_down(leaf_send[None], leaf_update, (empty_sum, empty_sum))
    sep_total = reduce_row(sep_part, rhs_cols)
    sep_y = lower_apply(sep_inv[0, 0, 0], sep_rhs[0, 0, 0].astype(jnp.float32) - sep_total)
    sep_send = sep_y.astype(jnp.bfloat16)

    def sep_update(totals, pieces, offset):
        how_many = pieces.shape[0]
        tile_block = cross_tiles.reshape(rows_out, how_many * tile_width)
        return totals + jnp.dot(
            tile_block,
            pieces.reshape(how_many * tile_width, rhs_cols),
            preferred_element_type=jnp.float32,
        )

    top_part = spread_down(sep_send[None], sep_update, top_part)
    top_total = reduce_row(add_sections(top_part), rhs_cols)
    top_y = lower_apply(top_inv[0, 0], top_rhs[0, 0].astype(jnp.float32) - top_total)
    top_x = upper_apply(top_inv[0, 0], top_y)
    top_flat = spread_across(top_x.astype(jnp.bfloat16)).reshape(rows_out, rhs_cols)
    cross_flat = cross_tiles.reshape(rows_out, row_count * tile_width)
    sep_flat_tiles = sep_tiles.reshape(rows_out, row_count * leaf_span)
    top_flat_tiles = top_tiles.reshape(rows_out, row_count * leaf_span)

    def sep_terms(offset, how_many):
        return lax.dot_general(cross_flat, top_flat, contract, preferred_element_type=jnp.float32)

    sep_t = collect_up(sep_terms, tile_width)
    sep_x = upper_apply(sep_inv[0, 0, 0], sep_y - sep_t)
    sep_row = spread_across(sep_x.astype(jnp.bfloat16)).reshape(rows_out, rhs_cols)

    def both_terms(offset, how_many):
        return lax.dot_general(
            sep_flat_tiles, sep_row, contract, preferred_element_type=jnp.float32
        ) + lax.dot_general(top_flat_tiles, top_flat, contract, preferred_element_type=jnp.float32)

    leaf_t = collect_up(both_terms, leaf_span)
    leaf_x = upper_apply(
        leaf_inv[0, 0, :, 0], leaf_y - leaf_t.reshape(leaf_count, tile_width, rhs_cols)
    )
    return (leaf_x[None, None, :, None], sep_x[None, None, None], top_x[None, None])


def solution(mesh):
    in_specs = (
        P("sec", "row", None, "col", None, None),
        P("sec", "row", "col", None, None),
        P("row", "col", None, None),
        P("sec", "row", None, "col", None, None),
        P("sec", "row", "col", None, None),
        P("row", "col", None, None),
        P("sec", "row", None, None, None, None, "col", None),
        P("sec", "row", None, None, None, None, "col", None),
        P("sec", "row", None, None, None, "col", None),
        P("sec", "row", None, None, None, "col"),
        P("sec", "row", None, None, None, "col"),
        P("sec", "row", None, None, "col"),
    )
    out_specs = (
        P("sec", "row", None, "col", None, None),
        P("sec", "row", "col", None, None),
        P("row", "col", None, None),
    )
    return jax.shard_map(body, mesh=mesh, in_specs=in_specs, out_specs=out_specs, check_vma=False)
```

profile of v0, /device:TPU:8, one launch (start us, length us, event | category | flops | bytes accessed | tf_op | source)
XLA Modules:
  0.0 758.6 jit_solution(15964059549455217081)
XLA Ops:
  7.2 0.0 reduce-scatter.5.cloned.1.call-start
  7.2 1.1 fusion.38
  8.3 12.6 %all-gather = bf16[512,256]{1,0:T(8,128)(2,1)S(1)} all-gather(bf16[128,256]{1,0:T(8,128)(2,1)S(1)} %get-tuple-element.6), channel_id=2, replica_groups=mesh['sec'=2,'row'=4,'col'=32] {'row'}, dimensions={0}, use_global_device_ids=true | all-gather | bytes 327680 | tf_op jit(solution)/shard_map/all_gather | solution.py:20
  20.9 0.7 convert_element_type.74
  21.6 0.1 copy.21
  21.7 6.0 broadcast_multiply_fusion.2
  27.7 7.2 mul.49
  34.9 5.4 fusion.17
  40.3 0.0 reduce-scatter.11.cloned.1.call-start
  40.4 0.6 copy-done.7
  41.0 0.1 copy.23
  41.1 0.1 copy.22
  41.2 4.0 broadcast_multiply_fusion
  45.3 3.3 fusion.5
  48.5 0.8 copy-done.1
  49.4 1.0 copy-done.2
  50.4 3.8 broadcast_multiply_fusion.1
  54.2 211.2 %reduce-scatter.5.cloned.1.call-done = f32[1,128,256]{2,1,0:T(8,128)} async-done(((f32[32,128,256]{2,1,0:T(8,128)}), f32[1,128,256]{2,1,0:T(8,128)}) %reduce-scatter.5.cloned.1.call-update) | async-done | bytes 131088 | tf_op jit(solution)/shard_map/reduce_scatter | solution.py:25
  265.4 1.3 fusion.39
  266.7 11.9 %all-gather.1 = bf16[512,256]{0,1:T(8,128)(2,1)S(1)} all-gather(bf16[128,256]{0,1:T(8,128)(2,1)S(1)} %get-tuple-element.8), channel_id=3, replica_groups=mesh['sec'=2,'row'=4,'col'=32] {'row'}, dimensions={0}, use_global_device_ids=true | all-gather | bytes 327680 | tf_op jit(solution)/shard_map/all_gather | solution.py:20
  278.6 6.7 convolution_add_fusion
  285.3 0.0 reduce-scatter.11.cloned.1.call-update
  285.3 0.0 all-reduce.2.cloned.1.call-start
  285.4 220.9 %reduce-scatter.11.cloned.1.call-done = f32[1,128,256]{2,1,0:T(8,128)} async-done(((f32[32,128,256]{2,1,0:T(8,128)}), f32[1,128,256]{2,1,0:T(8,128)}) %reduce-scatter.11.cloned.1.call-update) | async-done | bytes 131088 | tf_op jit(solution)/shard_map/reduce_scatter | solution.py:25
  506.3 0.0 all-reduce.2.cloned.1.call-update
  506.3 0.0 all-gather.7.cloned.1.call-start
  506.3 30.3 %all-reduce.2.cloned.1.call-done = f32[1,128,256]{2,1,0:T(8,128)} async-done(((f32[1,128,256]{2,1,0:T(8,128)}), f32[1,128,256]{2,1,0:T(8,128)}) %all-reduce.2.cloned.1.call-update) | async-done | bytes 131088 | tf_op jit(solution)/shard_map/psum | solution.py:35
  536.6 1.3 fusion.20
  537.9 0.9 bitcast_convert_fusion.1
  538.8 0.0 all-gather.7.cloned.1.call-update
  538.8 0.2 reduce-scatter.7.cloned.1.call-start
  539.1 76.2 %all-gather.7.cloned.1.call-done = bf16[4096,256]{0,1:T(8,128)(2,1)} async-done(((bf16[128,256]{0,1:T(8,128)(2,1)}), bf16[4096,256]{0,1:T(8,128)(2,1)}) %all-gather.7.cloned.1.call-update) | async-done | bytes 2097168 | tf_op jit(solution)/shard_map/all_gather | solution.py:39
  615.2 5.0 fusion
  620.3 0.0 reduce-scatter.7.cloned.1.call-update
  620.3 0.0 all-gather.9.cloned.1.call-start
  620.3 23.6 %reduce-scatter.7.cloned.1.call-done = f32[128,256]{0,1:T(8,128)} async-done(((f32[512,256]{0,1:T(8,128)}), f32[128,256]{0,1:T(8,128)}) %reduce-scatter.7.cloned.1.call-update) | async-done | bytes 131088 | tf_op jit(solution)/shard_map/reduce_scatter | solution.py:43
  643.9 1.8 bitcast_convert_fusion
  645.7 0.0 all-gather.9.cloned.1.call-update
  645.7 0.0 reduce-scatter.9.cloned.1.call-start
  645.8 3.5 fusion.3
  649.3 71.8 %all-gather.9.cloned.1.call-done = bf16[4096,256]{0,1:T(8,128)(2,1)} async-done(((bf16[128,256]{0,1:T(8,128)(2,1)}), bf16[4096,256]{0,1:T(8,128)(2,1)}) %all-gather.9.cloned.1.call-update) | async-done | bytes 2097168 | tf_op jit(solution)/shard_map/all_gather | solution.py:39
  721.0 5.0 fusion.14
  726.1 0.0 reduce-scatter.9.cloned.1.call-update
  726.1 0.8 copy.20
  726.8 0.8 copy.19
  727.6 22.1 %reduce-scatter.9.cloned.1.call-done = f32[128,256]{1,0:T(8,128)} async-done(((f32[512,256]{1,0:T(8,128)}), f32[128,256]{1,0:T(8,128)}) %reduce-scatter.9.cloned.1.call-update) | async-done | bytes 131088 | tf_op jit(solution)/shard_map/reduce_scatter | solution.py:43
  749.7 1.3 convolution_bitcast_fusion
  751.0 0.8 copy.18
  (20 shorter events, 0.1 us)
Async XLA Ops:
  7.2 258.3 %copy-start = (f32[1,1,1,128,128]{4,3,2,1,0:T(8,128)S(1)}, f32[1,1,1,128,128]{4,3,2,1,0:T(8,128)}, u32[]{:S(2)}) copy-start(f32[1,1,1,128,128]{4,3,2,1,0:T(8,128)} %param.16) | copy-start | bytes 196612
  7.2 258.2 %reduce-scatter.5.cloned.1.call-start = ((), (), s32[]{:S(2)}) async-start(), calls=%async_computation.4 | async-start | bytes 4325376 | tf_op jit(solution)/shard_map/reduce_scatter | solution.py:25
  40.3 0.7 copy-start.7
  40.3 0.8 copy-start.8
  40.3 465.9 %reduce-scatter.11.cloned.1.call-start = ((), (), s32[]{:S(2)}) async-start(), calls=%async_computation.9 | async-start | bytes 4325376 | tf_op jit(solution)/shard_map/reduce_scatter | solution.py:25
  45.2 4.1 copy-start.1
  45.3 5.1 copy-start.2
  50.4 215.1 %copy-start.5 = (bf16[1,1,1,128,256]{4,3,2,1,0:T(8,128)(2,1)S(1)}, bf16[1,1,1,128,256]{4,3,2,1,0:T(8,128)(2,1)}, u32[]{:S(2)}) copy-start(bf16[1,1,1,128,256]{4,3,2,1,0:T(8,128)(2,1)} %param.13) | copy-start | bytes 196612
  285.3 251.3 %copy-start.4 = (f32[1,1,128,128]{3,2,1,0:T(8,128)S(1)}, f32[1,1,128,128]{3,2,1,0:T(8,128)}, u32[]{:S(2)}) copy-start(f32[1,1,128,128]{3,2,1,0:T(8,128)} %param.17) | copy-start | bytes 196612
  285.3 251.3 %copy-start.6 = (bf16[1,1,128,256]{3,2,1,0:T(8,128)(2,1)S(1)}, bf16[1,1,128,256]{3,2,1,0:T(8,128)(2,1)}, u32[]{:S(2)}) copy-start(bf16[1,1,128,256]{3,2,1,0:T(8,128)(2,1)} %param.14) | copy-start | bytes 196612
  285.3 251.3 %all-reduce.2.cloned.1.call-start = ((), (), s32[]{:S(2)}) async-start(), calls=%async_computation.10 | async-start | bytes 262144 | tf_op jit(solution)/shard_map/psum | solution.py:35
  506.3 109.0 %all-gather.7.cloned.1.call-start = ((), (), s32[]{:S(2)}) async-start(), calls=%async_computation.7 | async-start | bytes 2162688 | tf_op jit(solution)/shard_map/all_gather | solution.py:39
  538.8 105.1 %reduce-scatter.7.cloned.1.call-start = ((), (), s32[]{:S(2)}) async-start(), calls=%async_computation.5 | async-start | bytes 655360 | tf_op jit(solution)/shard_map/reduce_scatter | solution.py:43
  615.2 30.5 %copy-start.9 = (bf16[4096,256]{0,1:T(8,128)(2,1)S(1)}, bf16[4096,256]{0,1:T(8,128)(2,1)}, u32[]{:S(2)}) copy-start(bf16[4096,256]{0,1:T(8,128)(2,1)} %all-gather.7.cloned.1.call-done) | copy-start | bytes 6291460
  620.3 100.8 %all-gather.9.cloned.1.call-start = ((), (), s32[]{:S(2)}) async-start(), calls=%async_computation.8 | async-start | bytes 2162688 | tf_op jit(solution)/shard_map/all_gather | solution.py:39
  645.7 104.0 %reduce-scatter.9.cloned.1.call-start = ((), (), s32[]{:S(2)}) async-start(), calls=%async_computation.6 | async-start | bytes 655360 | tf_op jit(solution)/shard_map/reduce_scatter | solution.py:43
  721.0 28.7 %copy-start.3 = (f32[1,1,1,1,128,128]{5,4,3,2,1,0:T(8,128)S(1)}, f32[1,1,1,1,128,128]{5,4,3,2,1,0:T(8,128)}, u32[]{:S(2)}) copy-start(f32[1,1,1,1,128,128]{5,4,3,2,1,0:T(8,128)} %param.15) | copy-start | bytes 196612
Sparse Core Ops, SparseCore 0:
  40.4 224.9 reduce-scatter.4
  285.4 220.7 reduce-scatter.10
  508.8 27.7 all-reduce.1
  539.5 75.6 all-gather.6
  620.4 23.4 reduce-scatter.6
  646.8 74.1 all-gather.8
  726.2 23.4 reduce-scatter.8
where the time goes:
time: 759 us
  waiting for transfers between devices  656 us (86%)
  matrix products  36.5 us (5%)
  blocking collectives  24.5 us (3%)
  other arithmetic  14.6 us (2%)
  between operations  14.2 us (2%)
  local copies, waits for them, and re-layouts  12.3 us (2%)
    reduce_scatter x2, waiting for transfers between devices, reduce_row(): lax.psum_scatter(partial_value.reshape(col_count, partial_value.shape[0]...  432 us
    all_gather x2, waiting for transfers between devices, spread_across(): return lax.all_gather(values[None], 'col', axis=0, tiled=True)  148 us
    reduce_scatter x2, waiting for transfers between devices, collect_up(): lax.psum_scatter(term_fn(jnp.int32(0), row_span * lax.axis_size('row')),...  45.7 us
    psum x1, waiting for transfers between devices, add_sections(): return lax.psum(partial_value, 'sec')  30.3 us
    all_gather x2, blocking collectives, spread_down(): lax.all_gather(values, 'row', axis=0, tiled=True)  24.5 us
  transfers between devices with their start and end apart: 7, of which 7 were waited for; matrix products, arithmetic and copies ran while one was open for 2% of the time, Pallas kernels for 0%

commit v1 on v0

v1 whole, which is shorter than its diff:
```python
import functools

import jax
import jax.numpy as jnp
from jax import lax
from jax.experimental import pallas as pl
from jax.experimental.pallas import tpu as pltpu
from jax.sharding import PartitionSpec as P

MESH = pl.DeviceIdType.MESH
NY = 4
BF = jnp.bfloat16
F32 = jnp.float32
HI = lax.Precision.HIGHEST


def kernel(
    NX,
    NZ,
    leaf_rhs,
    sep_rhs,
    top_rhs,
    leaf_inv,
    sep_inv,
    top_inv,
    sl_hbm,
    tl_hbm,
    ts_hbm,
    sl_mask,
    tl_mask,
    ts_mask,
    leaf_out,
    sep_out,
    top_out,
    raw,
    tiles,
    select,
    leaf_y,
    sep_y,
    leaf_all,
    sep_all,
    part,
    top_part,
    swap_out,
    swap_in,
    fa_send,
    fa_recv,
    fb_send,
    fb_recv,
    fz_send,
    fz_recv,
    ta_send,
    ta_recv,
    tb_send,
    tb_recv,
    tz_send,
    tz_recv,
    top_full,
    top_all,
    sepx_all,
    acc_sep,
    acc_leaf,
    xr_send,
    xr_recv,
    load_sem,
    xg_ss,
    xg_rs,
    xr_ss,
    xr_rs,
    a_ss,
    a_rs,
    b_ss,
    b_rs,
    z_ss,
    z_rs,
    swap_ss,
    swap_rs,
    ga_ss,
    ga_rs,
    gb_ss,
    gb_rs,
    gz_ss,
    gz_rs,
    pair_ss,
    pair_rs,
    full_ss,
    full_rs,
):
    W = 128
    NC = NY * NZ
    s = lax.axis_index("sec")
    x = lax.axis_index("row")
    c = lax.axis_index("col")
    z = c // NY
    y = c % NY

    def col_of(yy, zz):
        return zz * NY + yy

    y_up = lax.rem(y + 1, NY)
    y_far = lax.rem(y + 2, NY)
    y_dn = lax.rem(y + 3, NY)
    to_up = (s, x, col_of(y_up, z))
    to_dn = (s, x, col_of(y_dn, z))
    to_pair = (1 - s, x, c)

    def to_x(o):
        return (s, lax.rem(x + o, NX), c)

    def to_z(zz):
        return (s, x, col_of(y, zz))

    def order(k):
        half = (k + 1) // 2
        return NZ // 2 + half * (1 - 2 * lax.rem(k, 2))

    def remote(src, dst, ss, rs, dev):
        return pltpu.make_async_remote_copy(
            src_ref=src,
            dst_ref=dst,
            send_sem=ss,
            recv_sem=rs,
            device_id=dev,
            device_id_type=MESH,
        )

    loads = [
        pltpu.make_async_copy(ref, raw.at[t], load_sem.at[t])
        for t, ref in enumerate((sl_hbm, tl_hbm, ts_hbm))
    ]
    for load in loads:
        load.start()

    barrier = pltpu.get_barrier_semaphore()

    def greet(dev):
        pl.semaphore_signal(barrier, inc=1, device_id=dev, device_id_type=MESH)

    greet(to_pair)
    for o in range(1, NX):
        greet(to_x(o))
    greet(to_up)
    greet(to_dn)
    for o in range(1, NZ):
        greet(to_z(lax.rem(z + o, NZ)))

    ly = jnp.dot(leaf_inv[...], leaf_rhs[...].astype(F32), precision=HI, preferred_element_type=F32)
    leaf_y[...] = ly
    leaf_all[x] = ly.astype(BF)

    pl.semaphore_wait(barrier, NX + NZ + 1)

    def x_gather(p, buf):
        return [
            remote(buf.at[x], buf.at[x], xg_ss.at[p, o], xg_rs.at[p, o], to_x(o))
            for o in range(1, NX)
        ]

    leaf_sends = x_gather(0, leaf_all)
    for copy in leaf_sends:
        copy.start()

    SB = 64
    rows_i = lax.broadcasted_iota(jnp.int32, (SB * NX, SB * NX), 0)
    cols_i = lax.broadcasted_iota(jnp.int32, (SB * NX, SB * NX), 1)
    wanted = lax.rem(rows_i, SB) * NX + rows_i // SB
    select[...] = jnp.where(cols_i == wanted, 1.0, 0.0).astype(BF)

    def prep(t, mask, lo, n):
        def unit(i, carry):
            cc = lo + i
            yy = lax.rem(cc, NY)
            zz = cc // NY
            for sub in range(W // SB):
                start = pl.multiple_of(cc * (W * NX) + sub * (SB * NX), SB * NX)
                block = raw[t, pl.ds(start, SB * NX), :]
                moved = jnp.dot(select[...], block, preferred_element_type=F32)
                row = pl.multiple_of(zz * W + sub * SB, SB)
                for r in range(NX):
                    keep = mask[r, 0, cc].astype(F32)
                    tiles[t, yy, pl.ds(row, SB), r * W : (r + 1) * W] = (
                        moved[r * SB : (r + 1) * SB] * keep
                    ).astype(BF)
            return carry

        lax.fori_loop(0, n, unit, 0)

    loads[0].wait()
    prep(0, sl_mask, 0, NC)

    for copy in leaf_sends:
        copy.wait()

    MB = min(512, NZ * W)

    def forward(t, values, yy, write):
        def block(i, carry):
            row = pl.multiple_of(i * MB, MB)
            out = jnp.dot(
                tiles[t, yy, pl.ds(row, MB), :],
                values[...].reshape(NX * W, 2 * W),
                preferred_element_type=F32,
            )
            write(row, out)
            return carry

        lax.fori_loop(0, NZ * W // MB, block, 0)

    def sep_dot(yy):
        def write(row, out):
            part[yy, pl.ds(row, MB), :] = out

        forward(0, leaf_all, yy, write)

    H = W // 2

    def reduce_col(p, chunk, start_more, work, a_s, a_r, b_s, b_r, z_s, z_r):
        def zp_of(k):
            return lax.rem(z + order(k), NZ)

        def a_copies(k):
            return (
                remote(a_s.at[k, 0:H], a_r.at[0, k], a_ss.at[p, 0, k], a_rs.at[p, 0, k], to_up),
                remote(a_s.at[k, H:W], a_r.at[1, k], a_ss.at[p, 1, k], a_rs.at[p, 1, k], to_dn),
            )

        def b_copies(k):
            return (
                remote(b_s.at[0, k], b_r.at[0, k], b_ss.at[p, 0, k], b_rs.at[p, 0, k], to_up),
                remote(b_s.at[1, k], b_r.at[1, k], b_ss.at[p, 1, k], b_rs.at[p, 1, k], to_dn),
            )

        def z_copy(k):
            return remote(z_s.at[k], z_r.at[k], z_ss.at[p, k], z_rs.at[p, k], to_z(zp_of(k)))

        def send_a(k):
            a_s[k] = chunk(y_far, zp_of(k), 0, W).astype(BF)
            for copy in a_copies(k):
                copy.start()

        def send_b(k):
            zp = zp_of(k)
            up, dn = a_copies(k)
            cup, cdn = b_copies(k)
            b_s[0, k, H:W] = chunk(y_up, zp, H, H).astype(BF)
            b_s[1, k, 0:H] = chunk(y_dn, zp, 0, H).astype(BF)
            up.wait_recv()
            b_s[0, k, 0:H] = (chunk(y_up, zp, 0, H) + a_r[0, k].astype(F32)).astype(BF)
            cup.start()
            dn.wait_recv()
            b_s[1, k, H:W] = (chunk(y_dn, zp, H, H) + a_r[1, k].astype(F32)).astype(BF)
            cdn.start()

        def total(k):
            for copy in b_copies(k):
                copy.wait_recv()
            return chunk(y, zp_of(k), 0, W) + b_r[0, k].astype(F32) + b_r[1, k].astype(F32)

        def send_z(k):
            z_s[k] = total(k).astype(BF)
            z_copy(k).start()

        send_a(0)
        send_a(1)
        start_more()

        def step(k, carry):
            @pl.when(k < NZ - 2)
            def _():
                send_a(k + 2)

            send_b(k)
            work(k)

            @pl.when(k >= 2)
            def _():
                send_z(k - 2)

            return carry

        lax.fori_loop(0, NZ, step, 0)
        send_z(NZ - 2)
        out = total(NZ - 1)
        for k in range(NZ - 1):
            z_copy(k).wait_recv()
            out = out + z_r[k].astype(F32)

        def drain():
            def one(k, carry):
                for copy in a_copies(k) + b_copies(k):
                    copy.wait_send()

                @pl.when(k < NZ - 1)
                def _():
                    z_copy(k).wait_send()

                return carry

            lax.fori_loop(0, NZ, one, 0)

        return out, drain

    sep_dot(y_far)

    def sep_more():
        sep_dot(y_up)
        sep_dot(y_dn)
        sep_dot(y)

    def sep_chunk(yy, zp, lo, n):
        return part[yy, pl.ds(pl.multiple_of(zp * W + lo, n), n), :]

    per = max(1, 2 * NC // NZ)
    split = NZ // 2

    def top_leaf_dot(yy):
        def write(row, out):
            top_part[0, yy, pl.ds(row, MB), :] = out[:, 0:W]
            top_part[1, yy, pl.ds(row, MB), :] = out[:, W : 2 * W]

        forward(1, leaf_all, yy, write)

    def sep_work(k):
        @pl.when(k == 0)
        def _():
            loads[1].wait()
            loads[2].wait()

        @pl.when(k < split)
        def _():
            prep(1, tl_mask, k * per, per)

        @pl.when(k >= split)
        def _():
            prep(2, ts_mask, (k - split) * per, per)

        @pl.when(k == split)
        def _():
            top_leaf_dot(y)
            top_leaf_dot(y_up)

        @pl.when(k == NZ - 1)
        def _():
            top_leaf_dot(y_dn)
            top_leaf_dot(y_far)

    sep_sum, drain_sep = reduce_col(
        0, sep_chunk, sep_more, sep_work, fa_send, fa_recv, fb_send, fb_recv, fz_send, fz_recv
    )
    sy = jnp.dot(
        sep_inv[...],
        sep_rhs[...].astype(F32) - sep_sum,
        precision=HI,
        preferred_element_type=F32,
    )
    sep_y[...] = sy
    sep_all[x] = sy.astype(BF)
    sep_sends = x_gather(1, sep_all)
    for copy in sep_sends:
        copy.start()
    drain_sep()
    for copy in sep_sends:
        copy.wait()

    order_y = (y_far, y_up, y_dn, y)

    def swap_copy(i):
        return remote(
            swap_out.at[i], swap_in.at[i], swap_ss.at[i], swap_rs.at[i], to_pair
        )

    for i, yy in enumerate(order_y):

        def write(row, out, i=i, yy=yy):
            top_part[0, yy, pl.ds(row, MB), :] += out[:, 0:W]
            top_part[1, yy, pl.ds(row, MB), :] += out[:, W : 2 * W]
            swap_out[i, pl.ds(row, MB), :] = top_part[1 - s, yy, pl.ds(row, MB), :].astype(BF)

        forward(2, sep_all, yy, write)
        swap_copy(i).start()

    def join(i, yy):
        swap_copy(i).wait()

        def block(j, carry):
            row = pl.multiple_of(j * W, W)
            top_part[s, yy, pl.ds(row, W), :] += swap_in[i, pl.ds(row, W), :].astype(F32)
            return carry

        lax.fori_loop(0, NZ, block, 0)

    join(0, y_far)

    def top_more():
        join(1, y_up)
        join(2, y_dn)
        join(3, y)

    def top_chunk(yy, zp, lo, n):
        return top_part[s, yy, pl.ds(pl.multiple_of(zp * W + lo, n), n), :]

    top_sum, drain_top = reduce_col(
        1, top_chunk, top_more, lambda k: None, ta_send, ta_recv, tb_send, tb_recv, tz_send, tz_recv
    )
    mine = pl.ds(pl.multiple_of(s * W, W), W)
    ty = jnp.dot(
        top_inv[...],
        top_rhs[:, mine].astype(F32) - top_sum,
        precision=HI,
        preferred_element_type=F32,
    )
    tx = jnp.dot(ty.T, top_inv[...], precision=HI, preferred_element_type=F32)
    top_full[mine, :] = tx
    top_all[y, z, mine, :] = tx.astype(BF)

    def gather_col(p, buf, lo, rows, start_more, arrived, use):
        def zp_of(k):
            return lax.rem(z + NZ - order(NZ - 1 - k), NZ)

        def at(yy, zz, first, n):
            return buf.at[yy, zz, pl.ds(pl.multiple_of(lo + first, n), n)]

        half = rows // 2

        def z_copy(k):
            ref = at(y, z, 0, rows)
            target = lax.rem(z + order(NZ - 1 - k), NZ)
            return remote(ref, ref, gz_ss.at[p, k], gz_rs.at[p, k], to_z(target))

        def z_arrival(k):
            ref = at(y, zp_of(k), 0, rows)
            target = lax.rem(z + order(NZ - 1 - k), NZ)
            return remote(ref, ref, gz_ss.at[p, k], gz_rs.at[p, k], to_z(target))

        def b_send(k):
            ref = at(y, zp_of(k), 0, rows)
            return (
                remote(ref, ref, gb_ss.at[p, 0, k], gb_rs.at[p, 0, k], to_up),
                remote(ref, ref, gb_ss.at[p, 1, k], gb_rs.at[p, 1, k], to_dn),
            )

        def b_arrival(k):
            from_dn = at(y_dn, zp_of(k), 0, rows)
            from_up = at(y_up, zp_of(k), 0, rows)
            return (
                remote(from_dn, from_dn, gb_ss.at[p, 0, k], gb_rs.at[p, 0, k], to_up),
                remote(from_up, from_up, gb_ss.at[p, 1, k], gb_rs.at[p, 1, k], to_dn),
            )

        def a_send(k):
            up = at(y_dn, zp_of(k), 0, half)
            dn = at(y_up, zp_of(k), half, half)
            return (
                remote(up, up, ga_ss.at[p, 0, k], ga_rs.at[p, 0, k], to_up),
                remote(dn, dn, ga_ss.at[p, 1, k], ga_rs.at[p, 1, k], to_dn),
            )

        def a_arrival(k):
            first = at(y_far, zp_of(k), 0, half)
            second = at(y_far, zp_of(k), half, half)
            return (
                remote(first, first, ga_ss.at[p, 0, k], ga_rs.at[p, 0, k], to_up),
                remote(second, second, ga_ss.at[p, 1, k], ga_rs.at[p, 1, k], to_dn),
            )

        def first_leg(k, wait):
            if wait:
                z_arrival(k).wait_recv()
            for copy in b_send(k):
                copy.start()
            arrived(y, 0, zp_of(k), k)

        def second_leg(k):
            got = b_arrival(k)
            go = a_send(k)
            got[0].wait_recv()
            go[0].start()
            got[1].wait_recv()
            go[1].start()
            arrived(y_dn, 3, zp_of(k), k)
            arrived(y_up, 1, zp_of(k), k)

        def last_leg(k):
            for copy in a_arrival(k):
                copy.wait_recv()
            arrived(y_far, 2, zp_of(k), k)

        first_leg(0, False)
        for k in range(1, NZ):
            z_copy(k).start()
        start_more()

        def step(k, carry):
            first_leg(k, True)
            second_leg(k - 1)

            @pl.when(k >= 2)
            def _():
                last_leg(k - 2)

            @pl.when(k >= 3)
            def _():
                use(zp_of(k - 3), k - 3)

            return carry

        lax.fori_loop(1, NZ, step, 0)
        second_leg(NZ - 1)
        last_leg(NZ - 2)
        if NZ > 2:
            use(zp_of(NZ - 3), NZ - 3)
        use(zp_of(NZ - 2), NZ - 2)
        last_leg(NZ - 1)
        use(zp_of(NZ - 1), NZ - 1)

        def drain():
            def one(k, carry):
                for copy in b_send(k) + a_send(k):
                    copy.wait_send()

                @pl.when(k >= 1)
                def _():
                    z_copy(k).wait_send()

                return carry

            lax.fori_loop(0, NZ, one, 0)

        return drain

    def backward(acc, buf, t, zz):
        for ya, yb in ((y, y_dn), (y_up, y_far)):
            left = jnp.concatenate([buf[ya, zz], buf[yb, zz]], axis=1)
            row = pl.ds(pl.multiple_of(zz * W, W), W)
            right = jnp.concatenate([tiles[t, ya, row, :], tiles[t, yb, row, :]], axis=0)
            acc[...] += jnp.dot(left, right, preferred_element_type=F32)

    other = pl.ds(pl.multiple_of((1 - s) * W, W), W)

    def pair_copy(yy, o, zz, k):
        ref = top_all.at[yy, zz, mine]
        return remote(ref, ref, pair_ss.at[o, k], pair_rs.at[o, k], to_pair)

    def pair_arrival(yy, o, zz, k):
        ref = top_all.at[yy, zz, other]
        return remote(ref, ref, pair_ss.at[o, k], pair_rs.at[o, k], to_pair)

    def top_arrived(yy, o, zz, k):
        pair_copy(yy, o, zz, k).start()

    full_copy = remote(
        top_full.at[mine], top_full.at[mine], full_ss.at[0], full_rs.at[0], to_pair
    )

    def top_start():
        full_copy.start()
        acc_sep[...] = jnp.zeros_like(acc_sep)
        acc_leaf[...] = jnp.zeros_like(acc_leaf)
        drain_top()

    def top_use(zz, k):
        for o, yy in enumerate((y, y_up, y_far, y_dn)):
            pair_arrival(yy, o, zz, k).wait_recv()
        backward(acc_sep, top_all, 2, zz)

    drain_gtop = gather_col(0, top_all, s * W, W, top_start, top_arrived, top_use)

    def x_reduce(p, acc):
        def copy(o):
            return remote(
                xr_send.at[p, o], xr_recv.at[p, o], xr_ss.at[p, o], xr_rs.at[p, o], to_x(o)
            )

        for o in range(1, NX):
            lane = pl.ds(pl.multiple_of(lax.rem(x + o, NX) * W, W), W)
            xr_send[p, o] = acc[:, lane].astype(BF)
            copy(o).start()
        out = acc[:, pl.ds(pl.multiple_of(x * W, W), W)]
        for o in range(1, NX):
            copy(o).wait_recv()
            out = out + xr_recv[p, o].astype(F32)

        def drain():
            for o in range(1, NX):
                copy(o).wait_send()

        return out, drain

    sep_t, drain_x0 = x_reduce(0, acc_sep)
    sx = jnp.dot(sep_y[...].T - sep_t, sep_inv[...], precision=HI, preferred_element_type=F32)
    sepx_all[y, z] = sx.astype(BF)

    def sep_start():
        sep_out[...] = sx
        drain_x0()
        drain_gtop()

        def one(k, carry):
            zz = lax.rem(z + NZ - order(NZ - 1 - k), NZ)
            for o, yy in enumerate((y, y_up, y_far, y_dn)):
                pair_copy(yy, o, zz, k).wait_send()
            return carry

        lax.fori_loop(0, NZ, one, 0)
        full_copy.wait()
        top_out[...] = top_full[...]

    def sep_use(zz, k):
        backward(acc_leaf, top_all, 1, zz)
        backward(acc_leaf, sepx_all, 0, zz)

    drain_gsep = gather_col(
        1, sepx_all, 0, 2 * W, sep_start, lambda yy, o, zz, k: None, sep_use
    )
    leaf_t, drain_x1 = x_reduce(1, acc_leaf)
    leaf_out[...] = jnp.dot(
        leaf_y[...].T - leaf_t, leaf_inv[...], precision=HI, preferred_element_type=F32
    )
    drain_gsep()
    drain_x1()


def body(
    leaf_rhs,
    sep_rhs,
    top_rhs,
    leaf_inv,
    sep_inv,
    top_inv,
    sep_leaf,
    top_leaf,
    top_sep,
    sep_leaf_mask,
    top_leaf_mask,
    top_sep_mask,
):
    W = 128
    R = leaf_rhs.shape[-1]
    NC = sep_leaf.shape[2]
    NX = sep_leaf.shape[4]
    NZ = NC // NY
    rows = NC * W * NX

    def pattern(mask):
        return mask.reshape(NC, NX).T.reshape(NX, 1, NC)

    vm = pl.BlockSpec(memory_space=pltpu.VMEM)
    sm = pl.BlockSpec(memory_space=pltpu.SMEM)
    hbm = pl.BlockSpec(memory_space=pl.ANY)
    dma = pltpu.SemaphoreType.DMA
    out = jax.ShapeDtypeStruct((R, W), F32)
    H = W // 2

    def stage(cols):
        return [
            pltpu.VMEM((NZ, W, cols), BF),
            pltpu.VMEM((2, NZ, H, cols), BF),
            pltpu.VMEM((2, NZ, W, cols), BF),
            pltpu.VMEM((2, NZ, W, cols), BF),
            pltpu.VMEM((NZ, W, cols), BF),
            pltpu.VMEM((NZ, W, cols), BF),
        ]

    scratch = (
        [
            pltpu.VMEM((3, rows, W), BF),
            pltpu.VMEM((3, NY, NZ * W, NX * W), BF),
            pltpu.VMEM((64 * NX, 64 * NX), BF),
            pltpu.VMEM((W, R), F32),
            pltpu.VMEM((W, R), F32),
            pltpu.VMEM((NX, W, R), BF),
            pltpu.VMEM((NX, W, R), BF),
            pltpu.VMEM((NY, NZ * W, R), F32),
            pltpu.VMEM((2, NY, NZ * W, W), F32),
            pltpu.VMEM((NY, NZ * W, W), BF),
            pltpu.VMEM((NY, NZ * W, W), BF),
        ]
        + stage(R)
        + stage(W)
        + [
            pltpu.VMEM((R, W), F32),
            pltpu.VMEM((NY, NZ, R, W), BF),
            pltpu.VMEM((NY, NZ, R, W), BF),
            pltpu.VMEM((R, NX * W), F32),
            pltpu.VMEM((R, NX * W), F32),
            pltpu.VMEM((2, NX, R, W), BF),
            pltpu.VMEM((2, NX, R, W), BF),
            dma((3,)),
        ]
        + [dma((2, NX))] * 4
        + [dma((2, 2, NZ))] * 4
        + [dma((2, NZ))] * 2
        + [dma((NY,))] * 2
        + [dma((2, 2, NZ))] * 4
        + [dma((2, NZ))] * 2
        + [dma((NY, NZ))] * 2
        + [dma((1,))] * 2
    )
    lx, sx, tx = pl.pallas_call(
        functools.partial(kernel, NX, NZ),
        out_shape=(out, out, out),
        in_specs=[vm] * 6 + [hbm] * 3 + [sm] * 3,
        out_specs=(vm, vm, vm),
        scratch_shapes=scratch,
        compiler_params=pltpu.CompilerParams(
            collective_id=0, has_side_effects=True, vmem_limit_bytes=62 * 1024 * 1024
        ),
    )(
        leaf_rhs.reshape(W, R),
        sep_rhs.reshape(W, R),
        top_rhs.reshape(W, R),
        leaf_inv.reshape(W, W),
        sep_inv.reshape(W, W),
        top_inv.reshape(W, W),
        sep_leaf.reshape(rows, W),
        top_leaf.reshape(rows, W),
        top_sep.reshape(rows, W),
        pattern(sep_leaf_mask),
        pattern(top_leaf_mask),
        pattern(top_sep_mask),
    )
    return (lx.T[None, None, None, None], sx.T[None, None, None], tx.T[None, None])


def solution(mesh):
    in_specs = (
        P("sec", "row", None, "col", None, None),
        P("sec", "row", "col", None, None),
        P("row", "col", None, None),
        P("sec", "row", None, "col", None, None),
        P("sec", "row", "col", None, None),
        P("row", "col", None, None),
        P("sec", "row", None, None, None, None, "col", None),
        P("sec", "row", None, None, None, None, "col", None),
        P("sec", "row", None, None, None, "col", None),
        P("sec", "row", None, None, None, "col"),
        P("sec", "row", None, None, None, "col"),
        P("sec", "row", None, None, "col"),
    )
    out_specs = (
        P("sec", "row", None, "col", None, None),
        P("sec", "row", "col", None, None),
        P("row", "col", None, None),
    )
    return jax.shard_map(body, mesh=mesh, in_specs=in_specs, out_specs=out_specs, check_vma=False)
```

time: 759 us -> 147 us (0.19)
  waiting for transfers between devices: 656 us -> 0 us
  Pallas kernels: 0 us -> 141 us
  matrix products: 36.5 us -> 0 us
  blocking collectives: 24.5 us -> 0 us
  other arithmetic: 14.6 us -> 0 us
  between operations: 14.2 us -> 0.64 us
    reduce_scatter x4 -> x0, waiting for transfers between devices: 478 us -> none  [the longest x2 432 us: reduce_row(): lax.psum_scatter(partial_value.reshape(col_count, partial_value.shape[0]...]
    all_gather x2 -> x0, waiting for transfers between devices: 148 us -> none  [spread_across(): return lax.all_gather(values[None], 'col', axis=0, tiled=True)]
    pallas_call x0 -> x1, Pallas kernels: none -> 141 us  [body(): pl.pallas_call(functools.partial(kernel, NX, NZ), out_shape=(out, out, ou...]
    dot_general x12 -> x0, matrix products: 36.5 us -> none  [the longest x1 6.7 us: sep_update(): jnp.dot(tile_block, pieces.reshape(how_many * tile_width, rhs_cols), pref...]
    psum x1 -> x0, waiting for transfers between devices: 30.3 us -> none  [add_sections(): return lax.psum(partial_value, 'sec')]
    all_gather x2 -> x0, blocking collectives: 24.5 us -> none  [spread_down(): lax.all_gather(values, 'row', axis=0, tiled=True)]
    mul x3 -> x0, other arithmetic: 13.9 us -> none  [the longest x2 10 us: mask_tiles(): return tile_set * pattern.astype(jnp.bfloat16)[:, None, :, :, None]]
  transfers between devices with their start and end apart: 7 -> 0, of which waited for: 7 -> 0; matrix products, arithmetic and copies ran while one was open for 2% -> 0% of each run, Pallas kernels for 0% -> 0%
where the time goes in v1:
time: 147 us
  Pallas kernels  141 us (96%)
  local copies, waits for them, and re-layouts  4.98 us (3%)
    pallas_call x1, Pallas kernels, body(): pl.pallas_call(functools.partial(kernel, NX, NZ), out_shape=(out, out, ou...  141 us
    unnamed x3, local copies, waits for them, and re-layouts  4.98 us

profile of v1, /device:TPU:8, one launch (start us, length us, event | category | flops | bytes accessed | tf_op | source)
XLA Modules:
  0.0 146.9 jit_solution(16900973571347907025)
XLA Ops:
  0.6 141.3 %shard_map.139 = (f32[256,128]{1,0:T(8,128)}, f32[256,128]{1,0:T(8,128)}, f32[256,128]{1,0:T(8,128)}) custom-call(bf16[128,256]{1,0:T(8,128)(2,1)} %bitcast.45, bf16[128,256]{1,0:T(8,128)(2,1)} %bitcast.46, bf16[128,256]{1,0:T(8,128)(2,1)} %bitcast.47, f32[128,128]{1,0:T(8,128)} %bitcast.48, f32[128,128]{1,0:T(8,128)} %bitcast.49, f32[128,128]{1,0:T(8,128)} %bitcast.50, ...), custom_call_target="tpu_custom_call" | custom-call | tf_op jit(solution)/shard_map/pallas_call | solution.py:699
  141.9 1.7 %copy.18 = f32[1,1,1,1,128,256]{5,4,3,2,1,0:T(8,128)} copy(f32[1,1,1,1,128,256]{4,5,3,2,1,0:T(8,128)} %bitcast.44) | data formatting | bytes 262144
  143.6 1.7 %copy.19 = f32[1,1,1,128,256]{4,3,2,1,0:T(8,128)} copy(f32[1,1,1,128,256]{3,4,2,1,0:T(8,128)} %bitcast.43) | data formatting | bytes 262144
  145.3 1.7 %copy.20 = f32[1,1,128,256]{3,2,1,0:T(8,128)} copy(f32[1,1,128,256]{2,3,1,0:T(8,128)} %bitcast.42) | data formatting | bytes 262144

commit v2 on v1

--- a/solution.py
+++ b/solution.py
@@ -17,21 +17,30 @@
 def kernel(
     NX,
     NZ,
+    leaf_rhs_hbm,
+    sep_rhs_hbm,
+    top_rhs_hbm,
+    leaf_inv_hbm,
+    sep_inv_hbm,
+    top_inv_hbm,
+    sl_hbm,
+    tl_hbm,
+    ts_hbm,
+    sl_mask_hbm,
+    tl_mask_hbm,
+    ts_mask_hbm,
+    leaf_out,
+    sep_out,
+    top_out,
     leaf_rhs,
     sep_rhs,
     top_rhs,
     leaf_inv,
     sep_inv,
     top_inv,
-    sl_hbm,
-    tl_hbm,
-    ts_hbm,
     sl_mask,
     tl_mask,
     ts_mask,
-    leaf_out,
-    sep_out,
-    top_out,
     raw,
     tiles,
     select,
@@ -63,6 +72,7 @@
     xr_send,
     xr_recv,
     load_sem,
+    small_sem,
     xg_ss,
     xg_rs,
     xr_ss,
@@ -128,7 +138,26 @@
         pltpu.make_async_copy(ref, raw.at[t], load_sem.at[t])
         for t, ref in enumerate((sl_hbm, tl_hbm, ts_hbm))
     ]
-    for load in loads:
+    small = [
+        pltpu.make_async_copy(src, dst, small_sem.at[i])
+        for i, (src, dst) in enumerate(
+            (
+                (leaf_rhs_hbm, leaf_rhs),
+                (leaf_inv_hbm, leaf_inv),
+                (sl_mask_hbm, sl_mask),
+                (sep_rhs_hbm, sep_rhs),
+                (sep_inv_hbm, sep_inv),
+                (top_rhs_hbm, top_rhs),
+                (top_inv_hbm, top_inv),
+                (tl_mask_hbm, tl_mask),
+                (ts_mask_hbm, ts_mask),
+            )
+        )
+    ]
+    for load in small[0:3]:
+        load.start()
+    loads[0].start()
+    for load in small[3:]:
         load.start()
 
     barrier = pltpu.get_barrier_semaphore()
@@ -144,6 +173,8 @@
     for o in range(1, NZ):
         greet(to_z(lax.rem(z + o, NZ)))
 
+    small[0].wait()
+    small[1].wait()
     ly = jnp.dot(leaf_inv[...], leaf_rhs[...].astype(F32), precision=HI, preferred_element_type=F32)
     leaf_y[...] = ly
     leaf_all[x] = ly.astype(BF)
@@ -171,21 +202,28 @@
             cc = lo + i
             yy = lax.rem(cc, NY)
             zz = cc // NY
-            for sub in range(W // SB):
-                start = pl.multiple_of(cc * (W * NX) + sub * (SB * NX), SB * NX)
-                block = raw[t, pl.ds(start, SB * NX), :]
-                moved = jnp.dot(select[...], block, preferred_element_type=F32)
-                row = pl.multiple_of(zz * W + sub * SB, SB)
-                for r in range(NX):
-                    keep = mask[r, 0, cc].astype(F32)
+            start = pl.multiple_of(cc * (W * NX), W * NX)
+            block = jnp.concatenate(
+                [raw[t, pl.ds(start + sub * (SB * NX), SB * NX), :] for sub in range(W // SB)],
+                axis=1,
+            )
+            moved = jnp.dot(select[...], block, preferred_element_type=F32)
+            for r in range(NX):
+                keep = mask[r, 0, cc].astype(F32)
+                for sub in range(W // SB):
+                    row = pl.multiple_of(zz * W + sub * SB, SB)
                     tiles[t, yy, pl.ds(row, SB), r * W : (r + 1) * W] = (
-                        moved[r * SB : (r + 1) * SB] * keep
+                        moved[r * SB : (r + 1) * SB, sub * W : (sub + 1) * W] * keep
                     ).astype(BF)
             return carry
 
         lax.fori_loop(0, n, unit, 0)
 
+    for load in small[2:]:
+        load.wait()
     loads[0].wait()
+    loads[1].start()
+    loads[2].start()
     prep(0, sl_mask, 0, NC)
 
     for copy in leaf_sends:
@@ -260,14 +298,15 @@
             z_s[k] = total(k).astype(BF)
             z_copy(k).start()
 
-        send_a(0)
-        send_a(1)
+        ahead = min(3, NZ)
+        for k in range(ahead):
+            send_a(k)
         start_more()
 
         def step(k, carry):
-            @pl.when(k < NZ - 2)
+            @pl.when(k < NZ - ahead)
             def _():
-                send_a(k + 2)
+                send_a(k + ahead)
 
             send_b(k)
             work(k)
@@ -490,27 +529,31 @@
             z_copy(k).start()
         start_more()
 
+        behind = min(2, NZ - 1)
+
         def step(k, carry):
             first_leg(k, True)
-            second_leg(k - 1)
-
-            @pl.when(k >= 2)
+
+            @pl.when(k >= behind)
             def _():
-                last_leg(k - 2)
-
-            @pl.when(k >= 3)
+                second_leg(k - behind)
+
+            return carry
+
+        lax.fori_loop(1, NZ, step, 0)
+        for k in range(NZ - behind, NZ):
+            second_leg(k)
+
+        def finish(k, carry):
+            last_leg(k)
+
+            @pl.when(k >= 1)
             def _():
-                use(zp_of(k - 3), k - 3)
+                use(zp_of(k - 1), k - 1)
 
             return carry
 
-        lax.fori_loop(1, NZ, step, 0)
-        second_leg(NZ - 1)
-        last_leg(NZ - 2)
-        if NZ > 2:
-            use(zp_of(NZ - 3), NZ - 3)
-        use(zp_of(NZ - 2), NZ - 2)
-        last_leg(NZ - 1)
+        lax.fori_loop(0, NZ, finish, 0)
         use(zp_of(NZ - 1), NZ - 1)
 
         def drain():
@@ -645,8 +688,7 @@
         return mask.reshape(NC, NX).T.reshape(NX, 1, NC)
 
     vm = pl.BlockSpec(memory_space=pltpu.VMEM)
-    sm = pl.BlockSpec(memory_space=pltpu.SMEM)
-    hbm = pl.BlockSpec(memory_space=pl.ANY)
+    hbm = pl.BlockSpec(memory_space=pltpu.HBM)
     dma = pltpu.SemaphoreType.DMA
     out = jax.ShapeDtypeStruct((R, W), F32)
     H = W // 2
@@ -662,7 +704,10 @@
         ]
 
     scratch = (
-        [
+        [pltpu.VMEM((W, R), BF)] * 3
+        + [pltpu.VMEM((W, W), F32)] * 3
+        + [pltpu.SMEM((NX, 1, NC), jnp.int32)] * 3
+        + [
             pltpu.VMEM((3, rows, W), BF),
             pltpu.VMEM((3, NY, NZ * W, NX * W), BF),
             pltpu.VMEM((64 * NX, 64 * NX), BF),
@@ -686,6 +731,7 @@
             pltpu.VMEM((2, NX, R, W), BF),
             pltpu.VMEM((2, NX, R, W), BF),
             dma((3,)),
+            dma((9,)),
         ]
         + [dma((2, NX))] * 4
         + [dma((2, 2, NZ))] * 4
@@ -699,13 +745,16 @@
     lx, sx, tx = pl.pallas_call(
         functools.partial(kernel, NX, NZ),
         out_shape=(out, out, out),
-        in_specs=[vm] * 6 + [hbm] * 3 + [sm] * 3,
+        in_specs=[hbm] * 12,
         out_specs=(vm, vm, vm),
         scratch_shapes=scratch,
         compiler_params=pltpu.CompilerParams(
-            collective_id=0, has_side_effects=True, vmem_limit_bytes=62 * 1024 * 1024
+            collective_id=0, has_side_effects=True, vmem_limit_bytes=50 * 1024 * 1024
         ),
     )(
+        *(
+            pltpu.with_memory_space_constraint(v, pltpu.HBM)
+            for v in (
         leaf_rhs.reshape(W, R),
         sep_rhs.reshape(W, R),
         top_rhs.reshape(W, R),
@@ -718,6 +767,8 @@
         pattern(sep_leaf_mask),
         pattern(top_leaf_mask),
         pattern(top_sep_mask),
+            )
+        )
     )
     return (lx.T[None, None, None, None], sx.T[None, None, None], tx.T[None, None])
 

time: 147 us -> 130 us (0.88)
  Pallas kernels: 141 us -> 127 us
  local copies, waits for them, and re-layouts: 4.98 us -> 2.27 us
    pallas_call x1, Pallas kernels: 141 us -> 127 us  [body(): pl.pallas_call(functools.partial(kernel, NX, NZ), out_shape=(out, out, ou...]
    unnamed x3, local copies, waits for them, and re-layouts: 4.98 us -> 2.27 us
where the time goes in v2:
time: 130 us
  Pallas kernels  127 us (98%)
  local copies, waits for them, and re-layouts  2.27 us (2%)
    pallas_call x1, Pallas kernels, body(): pl.pallas_call(functools.partial(kernel, NX, NZ), out_shape=(out, out, ou...  127 us

profile of v2, /device:TPU:8, one launch (start us, length us, event | category | flops | bytes accessed | tf_op | source)
XLA Modules:
  0.0 129.9 jit_solution(212420392577648009)
XLA Ops:
  0.6 127.0 %shard_map.139 = (f32[256,128]{1,0:T(8,128)S(1)}, f32[256,128]{1,0:T(8,128)S(1)}, f32[256,128]{1,0:T(8,128)S(1)}) custom-call(bf16[128,256]{1,0:T(8,128)(2,1)} %bitcast.45, bf16[128,256]{1,0:T(8,128)(2,1)} %bitcast.46, bf16[128,256]{1,0:T(8,128)(2,1)} %bitcast.47, f32[128,128]{1,0:T(8,128)} %bitcast.48, f32[128,128]{1,0:T(8,128)} %bitcast.49, ...), custom_call_target="tpu_custom_call" | custom-call | tf_op jit(solution)/shard_map/pallas_call | solution.py:745
  127.6 0.8 copy.18
  128.3 0.8 copy.19
  129.1 0.8 copy.20

commit v3 on v2

--- a/solution.py
+++ b/solution.py
@@ -112,6 +112,7 @@
     y_dn = lax.rem(y + 3, NY)
     to_up = (s, x, col_of(y_up, z))
     to_dn = (s, x, col_of(y_dn, z))
+    to_far = (s, x, col_of(y_far, z))
     to_pair = (1 - s, x, c)
 
     def to_x(o):
@@ -170,6 +171,7 @@
         greet(to_x(o))
     greet(to_up)
     greet(to_dn)
+    greet(to_far)
     for o in range(1, NZ):
         greet(to_z(lax.rem(z + o, NZ)))
 
@@ -179,7 +181,7 @@
     leaf_y[...] = ly
     leaf_all[x] = ly.astype(BF)
 
-    pl.semaphore_wait(barrier, NX + NZ + 1)
+    pl.semaphore_wait(barrier, NX + NZ + 2)
 
     def x_gather(p, buf):
         return [
@@ -252,7 +254,7 @@
 
     H = W // 2
 
-    def reduce_col(p, chunk, start_more, work, a_s, a_r, b_s, b_r, z_s, z_r):
+    def reduce_col(p, ahead, lag, chunk, start_more, work, a_s, a_r, b_s, b_r, z_s, z_r):
         def zp_of(k):
             return lax.rem(z + order(k), NZ)
 
@@ -298,27 +300,31 @@
             z_s[k] = total(k).astype(BF)
             z_copy(k).start()
 
-        ahead = min(3, NZ)
+        ahead = min(ahead, NZ)
+        lag = min(lag, NZ - 1)
         for k in range(ahead):
             send_a(k)
         start_more()
 
         def step(k, carry):
-            @pl.when(k < NZ - ahead)
-            def _():
-                send_a(k + ahead)
+            if ahead < NZ:
+
+                @pl.when(k < NZ - ahead)
+                def _():
+                    send_a(k + ahead)
 
             send_b(k)
             work(k)
 
-            @pl.when(k >= 2)
+            @pl.when(k >= lag)
             def _():
-                send_z(k - 2)
+                send_z(k - lag)
 
             return carry
 
         lax.fori_loop(0, NZ, step, 0)
-        send_z(NZ - 2)
+        for k in range(max(0, NZ - lag), NZ - 1):
+            send_z(k)
         out = total(NZ - 1)
         for k in range(NZ - 1):
             z_copy(k).wait_recv()
@@ -384,7 +390,7 @@
             top_leaf_dot(y_far)
 
     sep_sum, drain_sep = reduce_col(
-        0, sep_chunk, sep_more, sep_work, fa_send, fa_recv, fb_send, fb_recv, fz_send, fz_recv
+        0, 4, 3, sep_chunk, sep_more, sep_work, fa_send, fa_recv, fb_send, fb_recv, fz_send, fz_recv
     )
     sy = jnp.dot(
         sep_inv[...],
@@ -408,9 +414,10 @@
             swap_out.at[i], swap_in.at[i], swap_ss.at[i], swap_rs.at[i], to_pair
         )
 
-    for i, yy in enumerate(order_y):
-
-        def write(row, out, i=i, yy=yy):
+    def top_dot(i):
+        yy = order_y[i]
+
+        def write(row, out):
             top_part[0, yy, pl.ds(row, MB), :] += out[:, 0:W]
             top_part[1, yy, pl.ds(row, MB), :] += out[:, W : 2 * W]
             swap_out[i, pl.ds(row, MB), :] = top_part[1 - s, yy, pl.ds(row, MB), :].astype(BF)
@@ -428,9 +435,13 @@
 
         lax.fori_loop(0, NZ, block, 0)
 
+    top_dot(0)
+    top_dot(1)
     join(0, y_far)
 
     def top_more():
+        top_dot(2)
+        top_dot(3)
         join(1, y_up)
         join(2, y_dn)
         join(3, y)
@@ -439,7 +450,7 @@
         return top_part[s, yy, pl.ds(pl.multiple_of(zp * W + lo, n), n), :]
 
     top_sum, drain_top = reduce_col(
-        1, top_chunk, top_more, lambda k: None, ta_send, ta_recv, tb_send, tb_recv, tz_send, tz_recv
+        1, 8, 5, top_chunk, top_more, lambda k: None, ta_send, ta_recv, tb_send, tb_recv, tz_send, tz_recv
     )
     mine = pl.ds(pl.multiple_of(s * W, W), W)
     ty = jnp.dot(
@@ -452,7 +463,11 @@
     top_full[mine, :] = tx
     top_all[y, z, mine, :] = tx.astype(BF)
 
-    def gather_col(p, buf, lo, rows, start_more, arrived, use):
+    def gather_col(p, buf, lo, rows, start_more, arrived, work, use, straight, behind, early):
+        straight = max(0, NZ - straight)
+        behind = min(behind, NZ - 1)
+        done = max(0, NZ - early)
+
         def zp_of(k):
             return lax.rem(z + NZ - order(NZ - 1 - k), NZ)
 
@@ -502,42 +517,78 @@
                 remote(second, second, ga_ss.at[p, 1, k], ga_rs.at[p, 1, k], to_dn),
             )
 
+        def far_send(k):
+            ref = at(y, zp_of(k), 0, rows)
+            return remote(ref, ref, ga_ss.at[p, 0, k], ga_rs.at[p, 0, k], to_far)
+
+        def far_arrival(k):
+            ref = at(y_far, zp_of(k), 0, rows)
+            return remote(ref, ref, ga_ss.at[p, 0, k], ga_rs.at[p, 0, k], to_far)
+
         def first_leg(k, wait):
             if wait:
                 z_arrival(k).wait_recv()
             for copy in b_send(k):
                 copy.start()
+
+            @pl.when(k >= straight)
+            def _():
+                far_send(k).start()
+
             arrived(y, 0, zp_of(k), k)
 
         def second_leg(k):
             got = b_arrival(k)
             go = a_send(k)
             got[0].wait_recv()
-            go[0].start()
+
+            @pl.when(k < straight)
+            def _():
+                go[0].start()
+
             got[1].wait_recv()
-            go[1].start()
+
+            @pl.when(k < straight)
+            def _():
+                go[1].start()
+
             arrived(y_dn, 3, zp_of(k), k)
             arrived(y_up, 1, zp_of(k), k)
 
         def last_leg(k):
-            for copy in a_arrival(k):
-                copy.wait_recv()
+            @pl.when(k < straight)
+            def _():
+                for copy in a_arrival(k):
+                    copy.wait_recv()
+
+            @pl.when(k >= straight)
+            def _():
+                far_arrival(k).wait_recv()
+
             arrived(y_far, 2, zp_of(k), k)
 
         first_leg(0, False)
         for k in range(1, NZ):
             z_copy(k).start()
         start_more()
-
-        behind = min(2, NZ - 1)
+        work(zp_of(0))
+
 
         def step(k, carry):
             first_leg(k, True)
+            work(zp_of(k))
 
             @pl.when(k >= behind)
             def _():
                 second_leg(k - behind)
 
+            if early < NZ:
+
+                @pl.when(k >= early)
+                def _():
+                    last_leg(k - early)
+                    use(zp_of(k - early), k - early)
+
             return carry
 
         lax.fori_loop(1, NZ, step, 0)
@@ -547,27 +598,34 @@
         def finish(k, carry):
             last_leg(k)
 
-            @pl.when(k >= 1)
+            @pl.when(k >= done + 1)
             def _():
                 use(zp_of(k - 1), k - 1)
 
             return carry
 
-        lax.fori_loop(0, NZ, finish, 0)
+        lax.fori_loop(done, NZ, finish, 0)
         use(zp_of(NZ - 1), NZ - 1)
 
         def drain():
             def one(k, carry):
-                for copy in b_send(k) + a_send(k):
+                for copy in b_send(k):
                     copy.wait_send()
 
-                @pl.when(k >= 1)
+                @pl.when(k < straight)
                 def _():
-                    z_copy(k).wait_send()
+                    for copy in a_send(k):
+                        copy.wait_send()
+
+                @pl.when(k >= straight)
+                def _():
+                    far_send(k).wait_send()
 
                 return carry
 
             lax.fori_loop(0, NZ, one, 0)
+            for k in range(1, NZ):
+                z_copy(k).wait_send()
 
         return drain
 
@@ -606,7 +664,10 @@
             pair_arrival(yy, o, zz, k).wait_recv()
         backward(acc_sep, top_all, 2, zz)
 
-    drain_gtop = gather_col(0, top_all, s * W, W, top_start, top_arrived, top_use)
+    def no_work(zz):
+        return None
+
+    drain_gtop = gather_col(0, top_all, s * W, W, top_start, top_arrived, no_work, top_use, 4, 4, NZ)
 
     def x_reduce(p, acc):
         def copy(o):
@@ -648,12 +709,14 @@
         full_copy.wait()
         top_out[...] = top_full[...]
 
+    def leaf_work(zz):
+        backward(acc_leaf, top_all, 1, zz)
+
     def sep_use(zz, k):
-        backward(acc_leaf, top_all, 1, zz)
         backward(acc_leaf, sepx_all, 0, zz)
 
     drain_gsep = gather_col(
-        1, sepx_all, 0, 2 * W, sep_start, lambda yy, o, zz, k: None, sep_use
+        1, sepx_all, 0, 2 * W, sep_start, lambda yy, o, zz, k: None, leaf_work, sep_use, 2, 2, 5
     )
     leaf_t, drain_x1 = x_reduce(1, acc_leaf)
     leaf_out[...] = jnp.dot(

time: 130 us -> 125 us (0.962)
  Pallas kernels: 127 us -> 122 us
    pallas_call x1, Pallas kernels: 127 us -> 122 us  [body(): pl.pallas_call(functools.partial(kernel, NX, NZ), out_shape=(out, out, ou...]
where the time goes in v3:
time: 125 us; the launch traced here: 124 us
  Pallas kernels  122 us (98%)
  local copies, waits for them, and re-layouts  2.27 us (2%)
    pallas_call x1, Pallas kernels, body(): pl.pallas_call(functools.partial(kernel, NX, NZ), out_shape=(out, out, ou...  122 us

profile of v3, /device:TPU:8, one launch (start us, length us, event | category | flops | bytes accessed | tf_op | source)
XLA Modules:
  0.0 124.5 jit_solution(298223694054711960)
XLA Ops:
  0.6 121.6 %shard_map.139 = (f32[256,128]{1,0:T(8,128)S(1)}, f32[256,128]{1,0:T(8,128)S(1)}, f32[256,128]{1,0:T(8,128)S(1)}) custom-call(bf16[128,256]{1,0:T(8,128)(2,1)} %bitcast.45, bf16[128,256]{1,0:T(8,128)(2,1)} %bitcast.46, bf16[128,256]{1,0:T(8,128)(2,1)} %bitcast.47, f32[128,128]{1,0:T(8,128)} %bitcast.48, f32[128,128]{1,0:T(8,128)} %bitcast.49, ...), custom_call_target="tpu_custom_call" | custom-call | tf_op jit(solution)/shard_map/pallas_call | solution.py:808
  122.2 0.8 copy.18
  123.0 0.8 copy.19
  123.7 0.8 copy.20

commit v4 on v3

--- a/solution.py
+++ b/solution.py
@@ -254,7 +254,7 @@
 
     H = W // 2
 
-    def reduce_col(p, ahead, lag, chunk, start_more, work, a_s, a_r, b_s, b_r, z_s, z_r):
+    def reduce_col(p, ahead, lag, chunk, start_more, work, late, a_s, a_r, b_s, b_r, z_s, z_r):
         def zp_of(k):
             return lax.rem(z + order(k), NZ)
 
@@ -325,6 +325,7 @@
         lax.fori_loop(0, NZ, step, 0)
         for k in range(max(0, NZ - lag), NZ - 1):
             send_z(k)
+        late()
         out = total(NZ - 1)
         for k in range(NZ - 1):
             z_copy(k).wait_recv()
@@ -384,13 +385,12 @@
             top_leaf_dot(y)
             top_leaf_dot(y_up)
 
-        @pl.when(k == NZ - 1)
-        def _():
-            top_leaf_dot(y_dn)
-            top_leaf_dot(y_far)
+    def sep_late():
+        top_leaf_dot(y_dn)
+        top_leaf_dot(y_far)
 
     sep_sum, drain_sep = reduce_col(
-        0, 4, 3, sep_chunk, sep_more, sep_work, fa_send, fa_recv, fb_send, fb_recv, fz_send, fz_recv
+        0, 4, 3, sep_chunk, sep_more, sep_work, sep_late, fa_send, fa_recv, fb_send, fb_recv, fz_send, fz_recv
     )
     sy = jnp.dot(
         sep_inv[...],
@@ -450,7 +450,7 @@
         return top_part[s, yy, pl.ds(pl.multiple_of(zp * W + lo, n), n), :]
 
     top_sum, drain_top = reduce_col(
-        1, 8, 5, top_chunk, top_more, lambda k: None, ta_send, ta_recv, tb_send, tb_recv, tz_send, tz_recv
+        1, 8, 5, top_chunk, top_more, lambda k: None, lambda: None, ta_send, ta_recv, tb_send, tb_recv, tz_send, tz_recv
     )
     mine = pl.ds(pl.multiple_of(s * W, W), W)
     ty = jnp.dot(

time: 125 us -> 126 us (level)
  no operation moved by 1% of the time
where the time goes in v4:
time: 126 us; the launch traced here: 125 us
  Pallas kernels  122 us (97%)
  local copies, waits for them, and re-layouts  2.27 us (2%)
    pallas_call x1, Pallas kernels, body(): pl.pallas_call(functools.partial(kernel, NX, NZ), out_shape=(out, out, ou...  122 us

profile of v4, /device:TPU:8, one launch (start us, length us, event | category | flops | bytes accessed | tf_op | source)
XLA Modules:
  0.0 125.2 jit_solution(2428081676481764452)
XLA Ops:
  0.6 122.3 %shard_map.139 = (f32[256,128]{1,0:T(8,128)S(1)}, f32[256,128]{1,0:T(8,128)S(1)}, f32[256,128]{1,0:T(8,128)S(1)}) custom-call(bf16[128,256]{1,0:T(8,128)(2,1)} %bitcast.45, bf16[128,256]{1,0:T(8,128)(2,1)} %bitcast.46, bf16[128,256]{1,0:T(8,128)(2,1)} %bitcast.47, f32[128,128]{1,0:T(8,128)} %bitcast.48, f32[128,128]{1,0:T(8,128)} %bitcast.49, ...), custom_call_target="tpu_custom_call" | custom-call | tf_op jit(solution)/shard_map/pallas_call | solution.py:808
  122.9 0.8 copy.18
  123.7 0.8 copy.19
  124.4 0.8 copy.20
